TPU v7x, 512 devices: a whole 4x4x16 slice. The times are simulated.
512 devices in a mesh: space: 64 (over y, z), spec: 8 (over x, core).
Axes of the slice: x: 4, y: 4, z: 16, core: 2. Of those that a mesh axis runs over, the one named last changes fastest.
Arguments:
- action: float32 [24, 36, 2048, 128], P('spec', None, 'space'), may hold values from 0.1 to 1
- courant: float32 [24], P('spec'), may hold values from 0.1 to 0.6
- bending: float32 [2048, 128], P('space'), may hold values from -0.25 to 0.25
- land_mask: int32 [2048, 128], P('space'), may hold values 0 or 1
- friction: float32 [2048, 128], P(('space', 'spec')), may hold values from 0.5 to 2
- wind_dir: float32 [2048, 128], P(('space', 'spec')), may hold values from -3.140625 to 3.140625
Outputs:
- wave_out: float32 [24, 36, 2048, 128], P('spec', None, 'space')
Inputs may be any that keep to these rules, and one draw needn't show every extreme that they name: `land_mask`: 1 marks land.
All inputs are finite; a program needn't handle non-finite values. No bound on the sum of `land_mask` on one device may be relied on, other than what follows from the above.
Results may differ from a plain program's by a relative error of at most 0.00002.
Values sent between devices are 32-bit elements; how exact they have to be, the bound alone decides.
No kernel may reach another device: no remote copies, remote signals or barrier semaphores. Data moves between devices by JAX's collectives and lax.ppermute only.
A program may use at most 64 MiB of HBM per device.

v0:
```python
import jax
import jax.numpy as jnp
from jax import lax
from jax.sharding import PartitionSpec as P

ITERS = 8


def padded(block, sides, width):
    for axis, dim in sides:
        count = lax.axis_size(axis)
        forward = [(i, i + 1) for i in range(count - 1)]
        forward.append((count - 1, 0))
        backward = [(target, source) for source, target in forward]
        low = lax.ppermute(
            lax.slice_in_dim(block, block.shape[dim] - width, None, axis=dim), axis, forward
        )
        high = lax.ppermute(lax.slice_in_dim(block, 0, width, axis=dim), axis, backward)
        block = jnp.concatenate([low, block, high], axis=dim)
    return block


def update_once(wide_x, speed_x, speed_y, turning, sea):
    center = wide_x[:, :, 1:-1]
    west = wide_x[:, :, :-2]
    east = wide_x[:, :, 2:]
    south = jnp.pad(center, ((0, 0), (0, 0), (0, 0), (1, 0)))[:, :, :, :-1]
    north = jnp.pad(center, ((0, 0), (0, 0), (0, 0), (0, 1)))[:, :, :, 1:]
    before = jnp.roll(center, 1, axis=1)
    after = jnp.roll(center, -1, axis=1)
    change = jnp.maximum(speed_x, 0.0) * (center - west) + jnp.minimum(speed_x, 0.0) * (
        east - center
    )
    change = (
        change
        + jnp.maximum(speed_y, 0.0) * (center - south)
        + jnp.minimum(speed_y, 0.0) * (north - center)
    )
    change = (
        change
        + jnp.maximum(turning, 0.0) * (center - before)
        + jnp.minimum(turning, 0.0) * (after - center)
    )
    return (center - change) * sea


def finish(values, lower, upper, ratio, energy, friction_here, dir_here, thetas):
    facing = jnp.maximum(jnp.cos(thetas[:, None, None] - dir_here[None]), 0.0)
    growth = 0.5 * friction_here[None, None] * ratio[:, None, None, None] * facing[None]
    coupling = 0.5 * (lower * upper - values * values)
    damping = 1.0 + 4.0 * (ratio * ratio)[:, None, None, None] * (energy * energy)[None, None]
    return (values * (1.0 + growth) + coupling) / damping


def shards(action, courant, bending, land_mask, friction, wind_dir):
    directions = action.shape[1]
    bands_here = action.shape[0]
    total_bands = bands_here * lax.axis_size("spec")
    sea = (1 - land_mask).astype(jnp.float32)
    thetas = 2.0 * jnp.pi * jnp.arange(directions).astype(jnp.float32) / directions
    speed_x = (courant[:, None] * jnp.cos(thetas)[None, :])[:, :, None, None]
    speed_y = (courant[:, None] * jnp.sin(thetas)[None, :])[:, :, None, None]
    state = action * sea[None, None]
    turning = (courant[:, None, None] * bending[None])[:, None]
    for substep in range(ITERS):
        wide_x = padded(state, (("space", 2),), 1)
        state = update_once(wide_x, speed_x, speed_y, turning, sea[None, None])
    points = lax.all_to_all(state, "spec", split_axis=2, concat_axis=0, tiled=True)
    energy = jnp.sum(points, axis=(0, 1)) / (total_bands * directions)
    ratio = (jnp.arange(total_bands).astype(jnp.float32) + 1.0) / total_bands
    stacked = jnp.pad(points, ((1, 1), (0, 0), (0, 0), (0, 0)))
    lower = jnp.roll(stacked[:-2], -1, axis=1)
    upper = jnp.roll(stacked[2:], 1, axis=1)
    finished = finish(points, lower, upper, ratio, energy, friction, wind_dir, thetas)
    return lax.all_to_all(finished, "spec", split_axis=0, concat_axis=2, tiled=True)


def solution(mesh):
    return jax.shard_map(
        shards,
        mesh=mesh,
        in_specs=(
            P("spec", None, "space", None),
            P("spec"),
            P("space", None),
            P("space", None),
            P(("space", "spec"), None),
            P(("space", "spec"), None),
        ),
        out_specs=P("spec", None, "space", None),
        check_vma=False,
    )
```

profile of v0, /device:TPU:1, one launch (start us, length us, event | category | flops | bytes accessed | tf_op | source)
XLA Modules:
  0.0 182.6 jit_solution(17031234568530258501)
XLA Ops:
  0.0 0.7 subtract_convert_fusion
  0.7 2.5 %copy_multiply_fusion = f32[3,36,32,128]{3,1,0,2:T(8,128)S(1)} fusion(f32[3,36,32,128]{3,2,1,0:T(8,128)} %param.6, f32[32,128]{1,0:T(8,128)S(1)} %subtract_convert_fusion), kind=kLoop, calls=%fused_computation.184 | loop fusion | flops 442368 | bytes 3555328 | tf_op jit(solution)/shard_map/mul | solution.py:63
  3.3 4.4 %collective-permute-start = (f32[3,36,1,128]{3,1,0,2:T(8,128)S(1)}, f32[3,36,1,128]{3,1,0,2:T(8,128)S(1)}, u32[]{:S(2)}, u32[]{:S(2)}) collective-permute-start(f32[3,36,1,128]{3,1,0,2:T(8,128)S(1)} %get-tuple-element.53), channel_id=1, source_target_pairs={{0,8},{8,16},{16,24},{24,32},{32,40},{40,48},{48,56},{56,64},{64,7... | collective-permute-start | bytes 165896 | tf_op jit(solution)/shard_map/ppermute | solution.py:15
  7.7 11.9 %collective-permute-start.1 = (f32[3,36,1,128]{3,1,0,2:T(8,128)S(1)}, f32[3,36,1,128]{3,1,0,2:T(8,128)S(1)}, u32[]{:S(2)}, u32[]{:S(2)}) collective-permute-start(f32[3,36,1,128]{3,1,0,2:T(8,128)S(1)} %get-tuple-element.54), channel_id=1, source_target_pairs={{8,0},{16,8},{24,16},{32,24},{40,32},{48,40},{56,48},{64,56},{72,6... | collective-permute-start | bytes 165896 | tf_op jit(solution)/shard_map/ppermute | solution.py:18
  19.6 0.3 fusion.163
  20.2 0.7 collective-permute-done.1
  20.9 2.1 %fusion.7 = f32[3,36,32,128]{3,1,0,2:T(8,128)S(1)} fusion(f32[3,36,32,128]{3,1,0,2:T(8,128)S(1)} %copy_multiply_fusion, f32[3,36,1,128]{3,1,0,2:T(8,128)S(1)} %collective-permute-done.1, f32[3,36,1,128]{3,1,0,2:T(8,128)S(1)} %collective-permute-done, f32[3,35,32,128]{3,1,0,2:T(8,128)S(1)} %get-tuple-element.50, f32[3,1,32,128]{3,1,0,2:T(1,128)S(1)} %get-tuple-element.52, ...), kind=kLoop, calls=%fused_computation.23 | loop fusion | flops 10174464 | bytes 7304896 | tf_op jit(solution)/shard_map/mul | solution.py:44
  23.0 0.3 fusion.160
  23.3 1.9 %collective-permute-start.2 = (f32[3,36,1,128]{3,1,0,2:T(8,128)S(1)}, f32[3,36,1,128]{3,1,0,2:T(8,128)S(1)}, u32[]{:S(2)}, u32[]{:S(2)}) collective-permute-start(f32[3,36,1,128]{3,1,0,2:T(8,128)S(1)} %get-tuple-element.47), channel_id=1, source_target_pairs={{0,8},{8,16},{16,24},{24,32},{32,40},{40,48},{48,56},{56,64},{64,7... | collective-permute-start | bytes 165896 | tf_op jit(solution)/shard_map/ppermute | solution.py:15
  25.3 7.0 %collective-permute-start.3 = (f32[3,36,1,128]{3,1,0,2:T(8,128)S(1)}, f32[3,36,1,128]{3,1,0,2:T(8,128)S(1)}, u32[]{:S(2)}, u32[]{:S(2)}) collective-permute-start(f32[3,36,1,128]{3,1,0,2:T(8,128)S(1)} %get-tuple-element.48), channel_id=1, source_target_pairs={{8,0},{16,8},{24,16},{32,24},{40,32},{48,40},{56,48},{64,56},{72,6... | collective-permute-start | bytes 165896 | tf_op jit(solution)/shard_map/ppermute | solution.py:18
  32.4 1.2 collective-permute-done.3
  33.6 2.1 %fusion.17 = f32[3,36,32,128]{3,1,0,2:T(8,128)S(1)} fusion(f32[3,36,32,128]{3,1,0,2:T(8,128)S(1)} %fusion.7, f32[3,36,1,128]{3,1,0,2:T(8,128)S(1)} %collective-permute-done.3, f32[3,36,1,128]{3,1,0,2:T(8,128)S(1)} %collective-permute-done.2, f32[3,35,32,128]{3,1,0,2:T(8,128)S(1)} %get-tuple-element.44, f32[3,1,32,128]{3,1,0,2:T(1,128)S(1)} %get-tuple-element.46, ...), kind=kLoop, calls=%fused_computation.33 | loop fusion | flops 10174464 | bytes 7304896 | tf_op jit(solution)/shard_map/mul | solution.py:44
  35.7 0.3 fusion.157
  36.0 1.9 %collective-permute-start.4 = (f32[3,36,1,128]{3,1,0,2:T(8,128)S(1)}, f32[3,36,1,128]{3,1,0,2:T(8,128)S(1)}, u32[]{:S(2)}, u32[]{:S(2)}) collective-permute-start(f32[3,36,1,128]{3,1,0,2:T(8,128)S(1)} %get-tuple-element.41), channel_id=1, source_target_pairs={{0,8},{8,16},{16,24},{24,32},{32,40},{40,48},{48,56},{56,64},{64,7... | collective-permute-start | bytes 165896 | tf_op jit(solution)/shard_map/ppermute | solution.py:15
  38.0 7.0 %collective-permute-start.5 = (f32[3,36,1,128]{3,1,0,2:T(8,128)S(1)}, f32[3,36,1,128]{3,1,0,2:T(8,128)S(1)}, u32[]{:S(2)}, u32[]{:S(2)}) collective-permute-start(f32[3,36,1,128]{3,1,0,2:T(8,128)S(1)} %get-tuple-element.42), channel_id=1, source_target_pairs={{8,0},{16,8},{24,16},{32,24},{40,32},{48,40},{56,48},{64,56},{72,6... | collective-permute-start | bytes 165896 | tf_op jit(solution)/shard_map/ppermute | solution.py:18
  45.1 1.2 collective-permute-done.5
  46.2 2.1 %fusion.27 = f32[3,36,32,128]{3,1,0,2:T(8,128)S(1)} fusion(f32[3,36,32,128]{3,1,0,2:T(8,128)S(1)} %fusion.17, f32[3,36,1,128]{3,1,0,2:T(8,128)S(1)} %collective-permute-done.5, f32[3,36,1,128]{3,1,0,2:T(8,128)S(1)} %collective-permute-done.4, f32[3,35,32,128]{3,1,0,2:T(8,128)S(1)} %get-tuple-element.38, f32[3,1,32,128]{3,1,0,2:T(1,128)S(1)} %get-tuple-element.40, ...), kind=kLoop, calls=%fused_computation.43 | loop fusion | flops 10174464 | bytes 7304896 | tf_op jit(solution)/shard_map/mul | solution.py:44
  48.4 0.3 fusion.154
  48.7 1.9 %collective-permute-start.6 = (f32[3,36,1,128]{3,1,0,2:T(8,128)S(1)}, f32[3,36,1,128]{3,1,0,2:T(8,128)S(1)}, u32[]{:S(2)}, u32[]{:S(2)}) collective-permute-start(f32[3,36,1,128]{3,1,0,2:T(8,128)S(1)} %get-tuple-element.35), channel_id=1, source_target_pairs={{0,8},{8,16},{16,24},{24,32},{32,40},{40,48},{48,56},{56,64},{64,7... | collective-permute-start | bytes 165896 | tf_op jit(solution)/shard_map/ppermute | solution.py:15
  50.6 7.0 %collective-permute-start.7 = (f32[3,36,1,128]{3,1,0,2:T(8,128)S(1)}, f32[3,36,1,128]{3,1,0,2:T(8,128)S(1)}, u32[]{:S(2)}, u32[]{:S(2)}) collective-permute-start(f32[3,36,1,128]{3,1,0,2:T(8,128)S(1)} %get-tuple-element.36), channel_id=1, source_target_pairs={{8,0},{16,8},{24,16},{32,24},{40,32},{48,40},{56,48},{64,56},{72,6... | collective-permute-start | bytes 165896 | tf_op jit(solution)/shard_map/ppermute | solution.py:18
  57.7 1.2 collective-permute-done.7
  58.9 2.1 %fusion.37 = f32[3,36,32,128]{3,1,0,2:T(8,128)S(1)} fusion(f32[3,36,32,128]{3,1,0,2:T(8,128)S(1)} %fusion.27, f32[3,36,1,128]{3,1,0,2:T(8,128)S(1)} %collective-permute-done.7, f32[3,36,1,128]{3,1,0,2:T(8,128)S(1)} %collective-permute-done.6, f32[3,35,32,128]{3,1,0,2:T(8,128)S(1)} %get-tuple-element.32, f32[3,1,32,128]{3,1,0,2:T(1,128)S(1)} %get-tuple-element.34, ...), kind=kLoop, calls=%fused_computation.53 | loop fusion | flops 10174464 | bytes 7304896 | tf_op jit(solution)/shard_map/mul | solution.py:44
  61.4 1.9 %collective-permute-start.8 = (f32[3,36,1,128]{3,1,0,2:T(8,128)S(1)}, f32[3,36,1,128]{3,1,0,2:T(8,128)S(1)}, u32[]{:S(2)}, u32[]{:S(2)}) collective-permute-start(f32[3,36,1,128]{3,1,0,2:T(8,128)S(1)} %get-tuple-element.29), channel_id=1, source_target_pairs={{0,8},{8,16},{16,24},{24,32},{32,40},{40,48},{48,56},{56,64},{64,7... | collective-permute-start | bytes 165896 | tf_op jit(solution)/shard_map/ppermute | solution.py:15
  63.3 7.0 %collective-permute-start.9 = (f32[3,36,1,128]{3,1,0,2:T(8,128)S(1)}, f32[3,36,1,128]{3,1,0,2:T(8,128)S(1)}, u32[]{:S(2)}, u32[]{:S(2)}) collective-permute-start(f32[3,36,1,128]{3,1,0,2:T(8,128)S(1)} %get-tuple-element.30), channel_id=1, source_target_pairs={{8,0},{16,8},{24,16},{32,24},{40,32},{48,40},{56,48},{64,56},{72,6... | collective-permute-start | bytes 165896 | tf_op jit(solution)/shard_map/ppermute | solution.py:18
  70.4 1.2 collective-permute-done.9
  71.6 2.1 %fusion.47 = f32[3,36,32,128]{3,1,0,2:T(8,128)S(1)} fusion(f32[3,36,32,128]{3,1,0,2:T(8,128)S(1)} %fusion.37, f32[3,36,1,128]{3,1,0,2:T(8,128)S(1)} %collective-permute-done.9, f32[3,36,1,128]{3,1,0,2:T(8,128)S(1)} %collective-permute-done.8, f32[3,35,32,128]{3,1,0,2:T(8,128)S(1)} %get-tuple-element.26, f32[3,1,32,128]{3,1,0,2:T(1,128)S(1)} %get-tuple-element.28, ...), kind=kLoop, calls=%fused_computation.63 | loop fusion | flops 10174464 | bytes 7304896 | tf_op jit(solution)/shard_map/mul | solution.py:44
  73.7 0.3 fusion.148
  74.1 1.9 %collective-permute-start.10 = (f32[3,36,1,128]{3,1,0,2:T(8,128)S(1)}, f32[3,36,1,128]{3,1,0,2:T(8,128)S(1)}, u32[]{:S(2)}, u32[]{:S(2)}) collective-permute-start(f32[3,36,1,128]{3,1,0,2:T(8,128)S(1)} %get-tuple-element.23), channel_id=1, source_target_pairs={{0,8},{8,16},{16,24},{24,32},{32,40},{40,48},{48,56},{56,64},{64,7... | collective-permute-start | bytes 165896 | tf_op jit(solution)/shard_map/ppermute | solution.py:15
  76.0 7.0 %collective-permute-start.11 = (f32[3,36,1,128]{3,1,0,2:T(8,128)S(1)}, f32[3,36,1,128]{3,1,0,2:T(8,128)S(1)}, u32[]{:S(2)}, u32[]{:S(2)}) collective-permute-start(f32[3,36,1,128]{3,1,0,2:T(8,128)S(1)} %get-tuple-element.24), channel_id=1, source_target_pairs={{8,0},{16,8},{24,16},{32,24},{40,32},{48,40},{56,48},{64,56},{72,6... | collective-permute-start | bytes 165896 | tf_op jit(solution)/shard_map/ppermute | solution.py:18
  83.1 1.2 collective-permute-done.11
  84.3 2.1 %fusion.57 = f32[3,36,32,128]{3,1,0,2:T(8,128)S(1)} fusion(f32[3,36,32,128]{3,1,0,2:T(8,128)S(1)} %fusion.47, f32[3,36,1,128]{3,1,0,2:T(8,128)S(1)} %collective-permute-done.11, f32[3,36,1,128]{3,1,0,2:T(8,128)S(1)} %collective-permute-done.10, f32[3,35,32,128]{3,1,0,2:T(8,128)S(1)} %get-tuple-element.20, f32[3,1,32,128]{3,1,0,2:T(1,128)S(1)} %get-tuple-element.22, ...), kind=kLoop, calls=%fused_computation.73 | loop fusion | flops 10174464 | bytes 7304896 | tf_op jit(solution)/shard_map/mul | solution.py:44
  86.4 0.3 fusion.145
  86.7 1.9 %collective-permute-start.12 = (f32[3,36,1,128]{3,1,0,2:T(8,128)S(1)}, f32[3,36,1,128]{3,1,0,2:T(8,128)S(1)}, u32[]{:S(2)}, u32[]{:S(2)}) collective-permute-start(f32[3,36,1,128]{3,1,0,2:T(8,128)S(1)} %get-tuple-element.17), channel_id=1, source_target_pairs={{0,8},{8,16},{16,24},{24,32},{32,40},{40,48},{48,56},{56,64},{64,7... | collective-permute-start | bytes 165896 | tf_op jit(solution)/shard_map/ppermute | solution.py:15
  88.7 7.0 %collective-permute-start.13 = (f32[3,36,1,128]{3,1,0,2:T(8,128)S(1)}, f32[3,36,1,128]{3,1,0,2:T(8,128)S(1)}, u32[]{:S(2)}, u32[]{:S(2)}) collective-permute-start(f32[3,36,1,128]{3,1,0,2:T(8,128)S(1)} %get-tuple-element.18), channel_id=1, source_target_pairs={{8,0},{16,8},{24,16},{32,24},{40,32},{48,40},{56,48},{64,56},{72,6... | collective-permute-start | bytes 165896 | tf_op jit(solution)/shard_map/ppermute | solution.py:18
  95.8 1.2 collective-permute-done.13
  97.0 2.1 %fusion.67 = f32[3,36,32,128]{3,1,0,2:T(8,128)S(1)} fusion(f32[3,36,32,128]{3,1,0,2:T(8,128)S(1)} %fusion.57, f32[3,36,1,128]{3,1,0,2:T(8,128)S(1)} %collective-permute-done.13, f32[3,36,1,128]{3,1,0,2:T(8,128)S(1)} %collective-permute-done.12, f32[3,35,32,128]{3,1,0,2:T(8,128)S(1)} %get-tuple-element.14, f32[3,1,32,128]{3,1,0,2:T(1,128)S(1)} %get-tuple-element.16, ...), kind=kLoop, calls=%fused_computation.83 | loop fusion | flops 10174464 | bytes 7304896 | tf_op jit(solution)/shard_map/mul | solution.py:44
  99.4 1.9 %collective-permute-start.14 = (f32[3,36,1,128]{3,1,0,2:T(8,128)S(1)}, f32[3,36,1,128]{3,1,0,2:T(8,128)S(1)}, u32[]{:S(2)}, u32[]{:S(2)}) collective-permute-start(f32[3,36,1,128]{3,1,0,2:T(8,128)S(1)} %get-tuple-element.11), channel_id=1, source_target_pairs={{0,8},{8,16},{16,24},{24,32},{32,40},{40,48},{48,56},{56,64},{64,7... | collective-permute-start | bytes 165896 | tf_op jit(solution)/shard_map/ppermute | solution.py:15
  101.3 7.0 %collective-permute-start.15 = (f32[3,36,1,128]{3,1,0,2:T(8,128)S(1)}, f32[3,36,1,128]{3,1,0,2:T(8,128)S(1)}, u32[]{:S(2)}, u32[]{:S(2)}) collective-permute-start(f32[3,36,1,128]{3,1,0,2:T(8,128)S(1)} %get-tuple-element.12), channel_id=1, source_target_pairs={{8,0},{16,8},{24,16},{32,24},{40,32},{48,40},{56,48},{64,56},{72,6... | collective-permute-start | bytes 165896 | tf_op jit(solution)/shard_map/ppermute | solution.py:18
  108.5 1.2 collective-permute-done.15
  109.6 3.5 %fusion.77 = f32[3,36,32,128]{3,1,0,2:T(8,128)} fusion(f32[3,36,32,128]{3,1,0,2:T(8,128)S(1)} %fusion.67, f32[3,36,1,128]{3,1,0,2:T(8,128)S(1)} %collective-permute-done.15, f32[3,36,1,128]{3,1,0,2:T(8,128)S(1)} %collective-permute-done.14, f32[3,35,32,128]{3,1,0,2:T(8,128)S(1)} %get-tuple-element.8, f32[3,1,32,128]{3,1,0,2:T(1,128)S(1)} %get-tuple-element.10, ...), kind=kLoop, calls=%fused_computation.93 | loop fusion | flops 10174464 | bytes 7304896 | tf_op jit(solution)/shard_map/mul | solution.py:44
  113.1 14.0 %all-to-all-start = ((f32[3,36,32,128]{3,1,0,2:T(8,128)}), f32[3,36,32,128]{3,1,0,2:T(8,128)S(1)}, u32[]{:S(2)}, u32[]{:S(2)}) async-start(f32[3,36,32,128]{3,1,0,2:T(8,128)} %fusion.77), calls=%async_computation | async-start | bytes 3932160 | tf_op jit(solution)/shard_map/all_to_all | solution.py:68
  127.3 0.6 cosine_maximum_fusion
  127.8 24.1 %all-to-all-done = f32[3,36,32,128]{3,1,0,2:T(8,128)S(1)} async-done(((f32[3,36,32,128]{3,1,0,2:T(8,128)}), f32[3,36,32,128]{3,1,0,2:T(8,128)S(1)}, u32[]{:S(2)}, u32[]{:S(2)}) %all-to-all-start) | async-done | bytes 1769504 | tf_op jit(solution)/shard_map/all_to_all | solution.py:68
  151.9 0.9 bitcast_reduce_fusion
  152.8 0.4 pad_slice_fusion.16
  153.4 1.3 fusion.139
  154.8 26.1 %all_to_all.36 = f32[24,36,4,128]{3,2,1,0:T(4,128)S(1)} all-to-all(f32[24,36,4,128]{3,2,1,0:T(4,128)S(1)} %fusion.139), channel_id=1, replica_groups=mesh['space'=64,'spec'=8] {'spec'}, dimensions={0} | all-to-all | bytes 3538944 | tf_op jit(solution)/shard_map/all_to_all | solution.py:75
  180.9 1.7 copy.12
  (45 shorter events, 1.7 us)
Async XLA Ops:
  3.3 17.0 %collective-permute-start = (f32[3,36,1,128]{3,1,0,2:T(8,128)S(1)}, f32[3,36,1,128]{3,1,0,2:T(8,128)S(1)}, u32[]{:S(2)}, u32[]{:S(2)}) collective-permute-start(f32[3,36,1,128]{3,1,0,2:T(8,128)S(1)} %get-tuple-element.53), channel_id=1, source_target_pairs={{0,8},{8,16},{16,24},{24,32},{32,40},{40,48},{48,56},{56,64},{64,7... | collective-permute-start | bytes 165896 | tf_op jit(solution)/shard_map/ppermute | solution.py:15
  7.6 12.4 %copy-start = (f32[32,128]{1,0:T(8,128)S(1)}, f32[32,128]{1,0:T(8,128)}, u32[]{:S(2)}) copy-start(f32[32,128]{1,0:T(8,128)} %param.8) | copy-start | bytes 49156
  7.6 12.4 %copy-start.1 = (f32[3]{0:T(128)S(1)}, f32[3]{0:T(128)}, u32[]{:S(2)}) copy-start(f32[3]{0:T(128)} %param.7) | copy-start | bytes 40
  7.7 13.2 %collective-permute-start.1 = (f32[3,36,1,128]{3,1,0,2:T(8,128)S(1)}, f32[3,36,1,128]{3,1,0,2:T(8,128)S(1)}, u32[]{:S(2)}, u32[]{:S(2)}) collective-permute-start(f32[3,36,1,128]{3,1,0,2:T(8,128)S(1)} %get-tuple-element.54), channel_id=1, source_target_pairs={{8,0},{16,8},{24,16},{32,24},{40,32},{48,40},{56,48},{64,56},{72,6... | collective-permute-start | bytes 165896 | tf_op jit(solution)/shard_map/ppermute | solution.py:18
  23.3 9.0 %collective-permute-start.2 = (f32[3,36,1,128]{3,1,0,2:T(8,128)S(1)}, f32[3,36,1,128]{3,1,0,2:T(8,128)S(1)}, u32[]{:S(2)}, u32[]{:S(2)}) collective-permute-start(f32[3,36,1,128]{3,1,0,2:T(8,128)S(1)} %get-tuple-element.47), channel_id=1, source_target_pairs={{0,8},{8,16},{16,24},{24,32},{32,40},{40,48},{48,56},{56,64},{64,7... | collective-permute-start | bytes 165896 | tf_op jit(solution)/shard_map/ppermute | solution.py:15
  25.3 8.3 %collective-permute-start.3 = (f32[3,36,1,128]{3,1,0,2:T(8,128)S(1)}, f32[3,36,1,128]{3,1,0,2:T(8,128)S(1)}, u32[]{:S(2)}, u32[]{:S(2)}) collective-permute-start(f32[3,36,1,128]{3,1,0,2:T(8,128)S(1)} %get-tuple-element.48), channel_id=1, source_target_pairs={{8,0},{16,8},{24,16},{32,24},{40,32},{48,40},{56,48},{64,56},{72,6... | collective-permute-start | bytes 165896 | tf_op jit(solution)/shard_map/ppermute | solution.py:18
  36.0 9.0 %collective-permute-start.4 = (f32[3,36,1,128]{3,1,0,2:T(8,128)S(1)}, f32[3,36,1,128]{3,1,0,2:T(8,128)S(1)}, u32[]{:S(2)}, u32[]{:S(2)}) collective-permute-start(f32[3,36,1,128]{3,1,0,2:T(8,128)S(1)} %get-tuple-element.41), channel_id=1, source_target_pairs={{0,8},{8,16},{16,24},{24,32},{32,40},{40,48},{48,56},{56,64},{64,7... | collective-permute-start | bytes 165896 | tf_op jit(solution)/shard_map/ppermute | solution.py:15
  38.0 8.3 %collective-permute-start.5 = (f32[3,36,1,128]{3,1,0,2:T(8,128)S(1)}, f32[3,36,1,128]{3,1,0,2:T(8,128)S(1)}, u32[]{:S(2)}, u32[]{:S(2)}) collective-permute-start(f32[3,36,1,128]{3,1,0,2:T(8,128)S(1)} %get-tuple-element.42), channel_id=1, source_target_pairs={{8,0},{16,8},{24,16},{32,24},{40,32},{48,40},{56,48},{64,56},{72,6... | collective-permute-start | bytes 165896 | tf_op jit(solution)/shard_map/ppermute | solution.py:18
  48.7 9.0 %collective-permute-start.6 = (f32[3,36,1,128]{3,1,0,2:T(8,128)S(1)}, f32[3,36,1,128]{3,1,0,2:T(8,128)S(1)}, u32[]{:S(2)}, u32[]{:S(2)}) collective-permute-start(f32[3,36,1,128]{3,1,0,2:T(8,128)S(1)} %get-tuple-element.35), channel_id=1, source_target_pairs={{0,8},{8,16},{16,24},{24,32},{32,40},{40,48},{48,56},{56,64},{64,7... | collective-permute-start | bytes 165896 | tf_op jit(solution)/shard_map/ppermute | solution.py:15
  50.6 8.3 %collective-permute-start.7 = (f32[3,36,1,128]{3,1,0,2:T(8,128)S(1)}, f32[3,36,1,128]{3,1,0,2:T(8,128)S(1)}, u32[]{:S(2)}, u32[]{:S(2)}) collective-permute-start(f32[3,36,1,128]{3,1,0,2:T(8,128)S(1)} %get-tuple-element.36), channel_id=1, source_target_pairs={{8,0},{16,8},{24,16},{32,24},{40,32},{48,40},{56,48},{64,56},{72,6... | collective-permute-start | bytes 165896 | tf_op jit(solution)/shard_map/ppermute | solution.py:18
  61.4 9.0 %collective-permute-start.8 = (f32[3,36,1,128]{3,1,0,2:T(8,128)S(1)}, f32[3,36,1,128]{3,1,0,2:T(8,128)S(1)}, u32[]{:S(2)}, u32[]{:S(2)}) collective-permute-start(f32[3,36,1,128]{3,1,0,2:T(8,128)S(1)} %get-tuple-element.29), channel_id=1, source_target_pairs={{0,8},{8,16},{16,24},{24,32},{32,40},{40,48},{48,56},{56,64},{64,7... | collective-permute-start | bytes 165896 | tf_op jit(solution)/shard_map/ppermute | solution.py:15
  63.3 8.3 %collective-permute-start.9 = (f32[3,36,1,128]{3,1,0,2:T(8,128)S(1)}, f32[3,36,1,128]{3,1,0,2:T(8,128)S(1)}, u32[]{:S(2)}, u32[]{:S(2)}) collective-permute-start(f32[3,36,1,128]{3,1,0,2:T(8,128)S(1)} %get-tuple-element.30), channel_id=1, source_target_pairs={{8,0},{16,8},{24,16},{32,24},{40,32},{48,40},{56,48},{64,56},{72,6... | collective-permute-start | bytes 165896 | tf_op jit(solution)/shard_map/ppermute | solution.py:18
  74.1 9.0 %collective-permute-start.10 = (f32[3,36,1,128]{3,1,0,2:T(8,128)S(1)}, f32[3,36,1,128]{3,1,0,2:T(8,128)S(1)}, u32[]{:S(2)}, u32[]{:S(2)}) collective-permute-start(f32[3,36,1,128]{3,1,0,2:T(8,128)S(1)} %get-tuple-element.23), channel_id=1, source_target_pairs={{0,8},{8,16},{16,24},{24,32},{32,40},{40,48},{48,56},{56,64},{64,7... | collective-permute-start | bytes 165896 | tf_op jit(solution)/shard_map/ppermute | solution.py:15
  76.0 8.3 %collective-permute-start.11 = (f32[3,36,1,128]{3,1,0,2:T(8,128)S(1)}, f32[3,36,1,128]{3,1,0,2:T(8,128)S(1)}, u32[]{:S(2)}, u32[]{:S(2)}) collective-permute-start(f32[3,36,1,128]{3,1,0,2:T(8,128)S(1)} %get-tuple-element.24), channel_id=1, source_target_pairs={{8,0},{16,8},{24,16},{32,24},{40,32},{48,40},{56,48},{64,56},{72,6... | collective-permute-start | bytes 165896 | tf_op jit(solution)/shard_map/ppermute | solution.py:18
  86.7 9.0 %collective-permute-start.12 = (f32[3,36,1,128]{3,1,0,2:T(8,128)S(1)}, f32[3,36,1,128]{3,1,0,2:T(8,128)S(1)}, u32[]{:S(2)}, u32[]{:S(2)}) collective-permute-start(f32[3,36,1,128]{3,1,0,2:T(8,128)S(1)} %get-tuple-element.17), channel_id=1, source_target_pairs={{0,8},{8,16},{16,24},{24,32},{32,40},{40,48},{48,56},{56,64},{64,7... | collective-permute-start | bytes 165896 | tf_op jit(solution)/shard_map/ppermute | solution.py:15
  88.7 8.3 %collective-permute-start.13 = (f32[3,36,1,128]{3,1,0,2:T(8,128)S(1)}, f32[3,36,1,128]{3,1,0,2:T(8,128)S(1)}, u32[]{:S(2)}, u32[]{:S(2)}) collective-permute-start(f32[3,36,1,128]{3,1,0,2:T(8,128)S(1)} %get-tuple-element.18), channel_id=1, source_target_pairs={{8,0},{16,8},{24,16},{32,24},{40,32},{48,40},{56,48},{64,56},{72,6... | collective-permute-start | bytes 165896 | tf_op jit(solution)/shard_map/ppermute | solution.py:18
  99.4 9.0 %collective-permute-start.14 = (f32[3,36,1,128]{3,1,0,2:T(8,128)S(1)}, f32[3,36,1,128]{3,1,0,2:T(8,128)S(1)}, u32[]{:S(2)}, u32[]{:S(2)}) collective-permute-start(f32[3,36,1,128]{3,1,0,2:T(8,128)S(1)} %get-tuple-element.11), channel_id=1, source_target_pairs={{0,8},{8,16},{16,24},{24,32},{32,40},{40,48},{48,56},{56,64},{64,7... | collective-permute-start | bytes 165896 | tf_op jit(solution)/shard_map/ppermute | solution.py:15
  101.3 8.3 %collective-permute-start.15 = (f32[3,36,1,128]{3,1,0,2:T(8,128)S(1)}, f32[3,36,1,128]{3,1,0,2:T(8,128)S(1)}, u32[]{:S(2)}, u32[]{:S(2)}) collective-permute-start(f32[3,36,1,128]{3,1,0,2:T(8,128)S(1)} %get-tuple-element.12), channel_id=1, source_target_pairs={{8,0},{16,8},{24,16},{32,24},{40,32},{48,40},{56,48},{64,56},{72,6... | collective-permute-start | bytes 165896 | tf_op jit(solution)/shard_map/ppermute | solution.py:18
  113.1 14.0 %copy-start.3 = (f32[4,128]{1,0:T(4,128)S(1)}, f32[4,128]{1,0:T(4,128)}, u32[]{:S(2)}) copy-start(f32[4,128]{1,0:T(4,128)} %param.10) | copy-start | bytes 6148
  113.1 14.2 %copy-start.2 = (f32[4,128]{1,0:T(4,128)S(1)}, f32[4,128]{1,0:T(4,128)}, u32[]{:S(2)}) copy-start(f32[4,128]{1,0:T(4,128)} %param.11) | copy-start | bytes 6148
  113.1 38.8 %all-to-all-start = ((f32[3,36,32,128]{3,1,0,2:T(8,128)}), f32[3,36,32,128]{3,1,0,2:T(8,128)S(1)}, u32[]{:S(2)}, u32[]{:S(2)}) async-start(f32[3,36,32,128]{3,1,0,2:T(8,128)} %fusion.77), calls=%async_computation | async-start | bytes 3932160 | tf_op jit(solution)/shard_map/all_to_all | solution.py:68
where the time goes:
time: 184 us; the launch traced here: 183 us
  starting transfers between devices  92.8 us (50%)
  waiting for transfers between devices  33 us (18%)
  blocking collectives  26.1 us (14%)
  other arithmetic  24.9 us (14%)
  local copies, waits for them, and re-layouts  5.16 us (3%)
    ppermute x8, starting transfers between devices, padded(): lax.ppermute(lax.slice_in_dim(block, 0, width, axis=dim), axis, backward)  61 us
    all_to_all x1, blocking collectives, shards(): lax.all_to_all(finished, 'spec', split_axis=0, concat_axis=2, tiled=True)  26.1 us
    all_to_all x1, waiting for transfers between devices, shards(): lax.all_to_all(state, 'spec', split_axis=2, concat_axis=0, tiled=True)  24.1 us
    mul x8, other arithmetic, update_once(): return (center - change) * sea  18.5 us
    ppermute x8, starting transfers between devices, padded(): lax.ppermute(lax.slice_in_dim(block, block.shape[dim] - width, None, axis...  17.8 us
    all_to_all x1, starting transfers between devices, shards(): lax.all_to_all(state, 'spec', split_axis=2, concat_axis=0, tiled=True)  14 us
    ppermute x8, waiting for transfers between devices, padded(): lax.ppermute(lax.slice_in_dim(block, 0, width, axis=dim), axis, backward)  8.94 us
  transfers between devices with their start and end apart: 17, of which 9 were waited for; matrix products, arithmetic and copies ran while one was open for 1% of the time, Pallas kernels for 0%

commit v1 on v0

v1 whole, which is shorter than its diff:
```python
import functools

import jax
import jax.numpy as jnp
import numpy as np
from jax import lax
from jax.experimental import pallas as pl
from jax.experimental.pallas import tpu as pltpu
from jax.sharding import PartitionSpec as P

ITERS = 8
DIRS = 36
COLS = 32
HALF = DIRS // 2
ANGLES = 2.0 * np.pi * np.arange(DIRS) / DIRS
COS = [float(v) for v in np.cos(ANGLES)]
SIN = [float(v) for v in np.sin(ANGLES)]
EASTGOING = [d for d in range(DIRS) if COS[d] > 0.0]
WESTGOING = [d for d in range(DIRS) if COS[d] <= 0.0]
NORTHGOING = [SIN[d] >= 0.0 for d in range(DIRS)]
SLAB = COLS + 2 * ITERS
ROWS1 = DIRS * SLAB
TILES = HALF + HALF // 2 - 2
SPAN = DIRS * 2 * ITERS
WHOLE = pl.BlockSpec(memory_space=pltpu.VMEM)
SCALARS = pl.BlockSpec(memory_space=pltpu.SMEM)
PARAMS = pltpu.CompilerParams(vmem_limit_bytes=24 << 20)


def halo_plan(full):
    first = [d for d in full if (d - 1) % DIRS not in full][0]
    last = (first + HALF - 1) % DIRS
    up = [(last + 1 + j) % DIRS for j in range(HALF // 2)]
    down = [(first - 1 - j) % DIRS for j in range(HALF // 2)]
    pairs = [(0, up[0], up[6]), (1, up[1], up[5]), (2, up[2], up[4]), (3, up[3], down[3])]
    pairs += [(0, down[0], down[6]), (1, down[1], down[5]), (2, down[2], down[4])]
    unused = [up[7], up[8], down[7], down[8]]
    return [(first + i) % DIRS for i in range(HALF)], pairs, unused


def pack_kernel(
    courant_ref, action_hbm, *refs
):
    maps_hbm, (to_east_ref, to_west_ref, speed_ref, action_ref), maps_ref, (sems,) = (
        refs[:4], refs[4:8], refs[8:12], refs[12:]
    )
    row = lax.broadcasted_iota(jnp.int32, (ITERS, 128), 0)
    bands = action_ref.shape[0]
    copies = [pltpu.make_async_copy(action_hbm.at[f], action_ref.at[f], sems.at[f]) for f in range(bands)]
    maps = [pltpu.make_async_copy(src, dst, sems.at[bands + i]) for i, (src, dst) in enumerate(zip(maps_hbm, maps_ref))]
    for copy in copies + maps:
        copy.start()
    for f in range(bands):
        speed_ref[f] = jnp.full((ITERS, 128), courant_ref[f], jnp.float32)
    sides = (
        (to_east_ref, EASTGOING, False, slice(COLS - ITERS, COLS)),
        (to_west_ref, WESTGOING, True, slice(0, ITERS)),
    )
    for f in range(bands):
        copies[f].wait()
        for dst, full, flip, edge in sides:
            whole, pairs, _ = halo_plan(full)
            for t, d in enumerate(whole):
                dst[f * TILES + t] = action_ref[f, d, edge]
            for t, (j, one, two) in enumerate(pairs):
                a, b = action_ref[f, one, edge], action_ref[f, two, edge]
                if flip:
                    tile = jnp.where(row < ITERS - 1 - j, a, pltpu.roll(b, ITERS - 1 - j, 0))
                else:
                    tile = jnp.where(row > j, a, pltpu.roll(b, j + 1, 0))
                dst[f * TILES + HALF + t] = tile
    for copy in maps:
        copy.wait()
    bend_ref, land_ref = maps_ref[:2]
    for dst, _, _, edge in sides:
        dst[bands * TILES] = bend_ref[edge]
        dst[bands * TILES + 1] = 1.0 - land_ref[edge].astype(jnp.float32)


def pack(courant, action, *maps):
    bands = action.shape[0]
    halo = (bands * TILES + 2, ITERS, 128)
    in_hbm = pl.BlockSpec(memory_space=pltpu.MemorySpace.HBM)
    outs = [jax.ShapeDtypeStruct(o, jnp.float32) for o in (halo, halo, (bands, ITERS, 128), action.shape)]
    outs += [jax.ShapeDtypeStruct(x.shape, x.dtype) for x in maps]
    return pl.pallas_call(
        pack_kernel,
        in_specs=[SCALARS] + [in_hbm] * 5,
        out_specs=[WHOLE] * 8,
        out_shape=outs,
        scratch_shapes=[pltpu.SemaphoreType.DMA((bands + 4,))],
        compiler_params=PARAMS,
        name="pack",
    )(courant, action, *maps)


def weights(speed, d, lane):
    row_w = jnp.where(lane == (0 if NORTHGOING[d] else 127), 0.0, speed * abs(SIN[d]))
    return 1.0 - speed * (abs(COS[d]) + abs(SIN[d])), speed * abs(COS[d]), row_w


def band_of(role):
    odd = lax.rem(lax.axis_index("spec"), 2)
    return jnp.where(role == 0, 2 * odd, jnp.where(role == 1, 2 - 2 * odd, 1))


def rowwise(d, here):
    return pltpu.roll(here, 1 if NORTHGOING[d] else 127, 1)


def inner_kernel(
    speed_ref, action_ref, bend_ref, land_ref, far_ref, near_ref, own_ref, left, right, total_ref,
    st, own_c, col_c, row_c,
):
    lane = lax.broadcasted_iota(jnp.int32, (ITERS, 128), 1)
    blocks = COLS // ITERS
    part = [slice(ITERS * i, ITERS * (i + 1)) for i in range(blocks)]
    inside = [slice(ITERS * (i + 1), ITERS * (i + 2)) for i in range(blocks)]
    total_ref[...] = jnp.zeros_like(total_ref)

    def one_role(role, carry):
        band = band_of(role)
        speed = speed_ref[band]
        turn, positive = [], []
        sea = [1.0 - land_ref[p].astype(jnp.float32) for p in part]
        for i in range(blocks):
            bend = bend_ref[part[i]]
            turn.append(jnp.abs(bend * speed) * sea[i])
            positive.append(bend > 0.0)
        for d in range(DIRS):
            own_w, col_w, row_w = weights(speed, d, lane)
            for i in range(blocks):
                own_c[d, part[i]] = own_w - turn[i]
                col_c[d, part[i]] = col_w * sea[i]
                row_c[d, part[i]] = row_w * sea[i]
                st[0, d, inside[i]] = action_ref[band, d, part[i]] * sea[i]

        def load(k, d, shift):
            return [st[k, d, slice(p.start + shift, p.stop + shift)] for p in inside]

        def substep(k, carry):
            before = load(k, DIRS - 1, 0)
            here = load(k, 0, 0)
            for d in range(DIRS):
                after = load(k, (d + 1) % DIRS, 0)
                upwind = load(k, d, -1 if d in EASTGOING else 1)
                for i in range(blocks):
                    kept = own_c[d, part[i]] * here[i] + turn[i] * jnp.where(positive[i], before[i], after[i])
                    moved = col_c[d, part[i]] * upwind[i] + row_c[d, part[i]] * rowwise(d, here[i])
                    st[k + 1, d, inside[i]] = kept + moved
                before, here = here, after
            return carry

        lax.fori_loop(0, ITERS, substep, 0)
        flat = st.reshape((ITERS + 1) * ROWS1, 128)
        lflat, rflat = left.at[role].reshape((ITERS + 1) * SPAN, 128), right.at[role].reshape((ITERS + 1) * SPAN, 128)
        for d in range(DIRS):
            base, strip = d * SLAB + ITERS, d * 2 * ITERS
            lflat[pl.ds(strip + ITERS, ITERS, stride=SPAN), :] = flat[pl.ds(base, ITERS, stride=ROWS1 + 1), :]
            rflat[pl.ds(strip + ITERS - 1, ITERS, stride=SPAN), :] = flat[
                pl.ds(base + COLS - 1, ITERS, stride=ROWS1 - 1), :
            ]
            if d in WESTGOING:
                lflat[pl.ds(strip + ITERS + 1, ITERS, stride=SPAN), :] = flat[
                    pl.ds(base + 1, ITERS, stride=ROWS1 + 1), :
                ]
            else:
                rflat[pl.ds(strip + ITERS - 2, ITERS, stride=SPAN), :] = flat[
                    pl.ds(base + COLS - 2, ITERS, stride=ROWS1 - 1), :
                ]
        for r, out in enumerate((far_ref, near_ref, own_ref)):

            @pl.when(role == r)
            def _(out=out):
                sums = [total_ref[p] for p in part[1:3]]
                for d in range(DIRS):
                    for i in range(2):
                        value = st[ITERS, d, inside[i + 1]]
                        out[d, part[i + 1]] = value
                        sums[i] = sums[i] + value
                for i in range(2):
                    total_ref[part[i + 1]] = sums[i]

        return carry

    lax.fori_loop(0, action_ref.shape[0], one_role, 0)


def inner(speed, action, bending, land_mask):
    bands = action.shape[0]
    state = (DIRS, COLS, 128)
    strip = (bands, ITERS + 1, DIRS, 2 * ITERS, 128)
    return pl.pallas_call(
        inner_kernel,
        in_specs=[WHOLE] * 4,
        out_specs=[WHOLE] * 6,
        out_shape=[jax.ShapeDtypeStruct(o, jnp.float32) for o in (state, state, state, strip, strip, (COLS, 128))],
        scratch_shapes=[pltpu.VMEM((ITERS + 1, DIRS, SLAB, 128), jnp.float32)]
        + [pltpu.VMEM((DIRS, COLS, 128), jnp.float32)] * 3,
        cost_estimate=pl.CostEstimate(flops=40_000_000, bytes_accessed=6_000_000, transcendentals=0),
        compiler_params=PARAMS,
        name="inner",
    )(speed, action, bending, land_mask)


def strips_kernel(
    speed_ref, west_ref, east_ref, bend_ref, land_ref, friction_ref, wind_ref,
    far_in, near_in, own_in, left_in, right_in, total_in,
    far_ref, near_ref, own_ref, left_all, right_all, total, pay_ref, own_c, col_c, row_c, sea_ext, bend_ext,
):
    lane = lax.broadcasted_iota(jnp.int32, (ITERS, 128), 1)
    bands = left_all.shape[0]
    extra = west_ref.shape[0] - 2
    bend_ext[:ITERS] = west_ref[extra]
    bend_ext[ITERS : ITERS + COLS] = bend_ref[...]
    bend_ext[ITERS + COLS :] = east_ref[extra]
    sea_ext[:ITERS] = west_ref[extra + 1]
    sea_ext[ITERS : ITERS + COLS] = 1.0 - land_ref[...].astype(jnp.float32)
    sea_ext[ITERS + COLS :] = east_ref[extra + 1]
    zero = jnp.zeros((ITERS, 128), jnp.float32)

    def one_role(role, carry):
        band = band_of(role)
        speed = speed_ref[band]
        left, right = left_all.at[role], right_all.at[role]
        for d in range(DIRS):
            own_c[d], col_c[d], row_c[d] = weights(speed, d, lane)
        for src, buf, full, flip, row0 in (
            (west_ref, left, EASTGOING, False, 0),
            (east_ref, right, WESTGOING, True, ITERS),
        ):
            whole, pairs, unused = halo_plan(full)
            sea = src[extra + 1]
            rows = slice(row0, row0 + ITERS)
            for t, d in enumerate(whole):
                buf[0, d, rows] = src[band * TILES + t] * sea
            for t, (j, one, two) in enumerate(pairs):
                tile = src[band * TILES + HALF + t]
                buf[0, one, rows] = tile * sea
                buf[0, two, rows] = pltpu.roll(tile, j + 1 if flip else ITERS - 1 - j, 0) * sea
            for d in unused:
                buf[0, d, rows] = zero

        for k in range(ITERS):
            sides = []
            for buf, center, row0, window in (
                (left, 1, 0, k + 1),
                (right, ITERS - 1, ITERS, ITERS + COLS - 1 - k),
            ):
                s = sea_ext[window : window + ITERS]
                bend = bend_ext[window : window + ITERS]
                turn = jnp.abs(bend * speed) * s
                load = functools.partial(lambda buf, d, at: buf[k, d, at : at + ITERS], buf)
                sides.append([buf, center, row0, s, turn, bend > 0.0, load, load(DIRS - 1, center), load(0, center)])
            for d in range(DIRS):
                own_w, col_w, row_w = own_c[d], col_c[d], row_c[d]
                for side in sides:
                    buf, center, row0, s, turn, positive, load, before, here = side
                    after = load((d + 1) % DIRS, center)
                    upwind = load(d, center + (-1 if d in EASTGOING else 1))
                    moved = own_w * here + col_w * upwind + row_w * rowwise(d, here)
                    new = s * moved + turn * (jnp.where(positive, before, after) - here)
                    buf[k + 1, d, row0 : row0 + ITERS] = new
                    side[7], side[8] = here, after

        ends = (slice(0, ITERS), slice(COLS - ITERS, COLS))
        for r, out in enumerate((far_ref, near_ref, own_ref)):

            @pl.when(role == r)
            def _(out=out):
                sums = [total[p] for p in ends]
                for d in range(DIRS):
                    for i, value in enumerate((left[ITERS, d, :ITERS], right[ITERS, d, ITERS:])):
                        out[d, ends[i]] = value
                        sums[i] = sums[i] + value
                for i in range(2):
                    total[ends[i]] = sums[i]

        return carry

    lax.fori_loop(0, bands, one_role, 0)
    quarter = friction_ref.shape[0]
    for peer in range(pay_ref.shape[0]):
        pay_ref[peer, :COLS] = total[...]
        pay_ref[peer, COLS : COLS + quarter] = friction_ref[...]
        pay_ref[peer, COLS + quarter :] = wind_ref[...]


def strips(speed, west, east, kept, bending, land_mask, friction, wind_dir, peers):
    pay = jax.ShapeDtypeStruct((peers, COLS + 2 * friction.shape[0], 128), jnp.float32)
    outs = pl.pallas_call(
        strips_kernel,
        in_specs=[WHOLE] * 13,
        out_specs=[WHOLE] * 7,
        out_shape=[jax.ShapeDtypeStruct(x.shape, x.dtype) for x in kept] + [pay],
        input_output_aliases={7 + i: i for i in range(6)},
        scratch_shapes=[
            pltpu.VMEM((DIRS, ITERS, 128), jnp.float32),
            pltpu.VMEM((DIRS, ITERS, 128), jnp.float32),
            pltpu.VMEM((DIRS, ITERS, 128), jnp.float32),
            pltpu.VMEM((COLS + 2 * ITERS, 128), jnp.float32),
            pltpu.VMEM((COLS + 2 * ITERS, 128), jnp.float32),
        ],
        compiler_params=PARAMS,
        name="strips",
    )(speed, west, east, bending, land_mask, friction, wind_dir, *kept)
    return outs[0], outs[1], outs[2], outs[6]


def finish_kernel(far_ref, near_ref, own_ref, far_in_ref, near_in_ref, pay_ref, out_hbm, out_ref, sems):
    peers = pay_ref.shape[0]
    here = lax.axis_index("spec")
    odd = lax.rem(here, 2)
    bands = out_ref.shape[0]
    total_bands = bands * peers
    row = lax.broadcasted_iota(jnp.int32, (ITERS, 128), 0)
    part = [slice(ITERS * i, ITERS * (i + 1)) for i in range(COLS // ITERS)]
    along, across, energy2 = [], [], []
    for i, p in enumerate(part):
        energy = pay_ref[0, p]
        for peer in range(1, peers):
            energy = energy + pay_ref[peer, p]
        energy = energy / float(total_bands * DIRS)
        energy2.append(4.0 * energy * energy)
        lower_half, upper_half = pay_ref[2 * i, COLS:], pay_ref[2 * i + 1, COLS:]
        friction = jnp.where(row < 4, lower_half, pltpu.roll(upper_half, 4, 0))
        wind = jnp.where(row < 4, pltpu.roll(lower_half, 4, 0), upper_half)
        along.append(friction * jnp.cos(wind))
        across.append(friction * jnp.sin(wind))
    chunk = DIRS // sems.shape[1]

    def send(f, c):
        at = pl.ds(c * chunk, chunk)
        return pltpu.make_async_copy(out_ref.at[f, at], out_hbm.at[f, at], sems.at[f, c])

    for parity in (0, 1):

        @pl.when(odd == parity)
        def _(step=2 * parity - 1, order=(2 * parity, 2 - 2 * parity, 1)):
            plan = []
            for band in order:
                g = (here * bands + band + 1).astype(jnp.float32) / float(total_bands)
                plan.append((band, g, [0.5 / (1.0 + (g * g) * e) for e in energy2]))
            for d in range(DIRS):
                plus, minus = (d + step) % DIRS, (d - step) % DIRS
                for i, p in enumerate(part):
                    facing = jnp.maximum(COS[d] * along[i] + SIN[d] * across[i], 0.0)
                    pairs = (
                        (far_ref[d, p], own_ref[plus, p] * far_in_ref[minus, p]),
                        (near_ref[d, p], own_ref[minus, p] * near_in_ref[plus, p]),
                        (own_ref[d, p], far_ref[minus, p] * near_ref[plus, p]),
                    )
                    for (value, product), (band, g, scale) in zip(pairs, plan):
                        out_ref[band, d, p] = (value * (2.0 + g * facing - value) + product) * scale[i]
                if d % chunk == chunk - 1:
                    for f in range(bands):
                        send(f, d // chunk).start()

    for f in range(bands):
        for c in range(sems.shape[1]):
            send(f, c).wait()


def finish(far, near, own, far_in, near_in, pay, bands):
    out = (bands, DIRS, COLS, 128)
    return pl.pallas_call(
        finish_kernel,
        in_specs=[WHOLE] * 6,
        out_specs=pl.BlockSpec(memory_space=pltpu.MemorySpace.HBM),
        out_shape=jax.ShapeDtypeStruct(out, jnp.float32),
        scratch_shapes=[pltpu.VMEM(out, jnp.float32), pltpu.SemaphoreType.DMA((bands, 4))],
        compiler_params=PARAMS,
        name="finish",
    )(far, near, own, far_in, near_in, pay)


def shards(action, courant, bending, land_mask, friction, wind_dir):
    bands = action.shape[0]
    peers = lax.axis_size("spec")
    tiles = lax.axis_size("space")
    in_hbm = lambda x: pltpu.with_memory_space_constraint(x, pltpu.MemorySpace.HBM)
    to_east, to_west, speed, action, bending, land_mask, friction, wind_dir = pack(
        *map(in_hbm, (courant, action, bending, land_mask, friction, wind_dir))
    )
    ring = [(i, (i + 1) % tiles) for i in range(tiles)]
    west = lax.ppermute(to_east, "space", ring)
    east = lax.ppermute(to_west, "space", [(b, a) for a, b in ring])
    kept = inner(speed, action, bending, land_mask)
    far, near, own, pay = strips(speed, west, east, kept, bending, land_mask, friction, wind_dir, peers)
    far_pairs = [(i, i + 1) for i in range(1, peers - 1, 2)]
    near_pairs = [(i, i + 1) for i in range(0, peers, 2)]
    far_in = lax.ppermute(far, "spec", far_pairs + [(b, a) for a, b in far_pairs])
    near_in = lax.ppermute(near, "spec", near_pairs + [(b, a) for a, b in near_pairs])
    pay = pltpu.with_memory_space_constraint(pay, pltpu.MemorySpace.VMEM)
    pay = lax.all_to_all(pay, "spec", split_axis=0, concat_axis=0, tiled=True)
    return finish(far, near, own, far_in, near_in, pay, bands)


def solution(mesh):
    return jax.shard_map(
        shards,
        mesh=mesh,
        in_specs=(
            P("spec", None, "space", None),
            P("spec"),
            P("space", None),
            P("space", None),
            P(("space", "spec"), None),
            P(("space", "spec"), None),
        ),
        out_specs=P("spec", None, "space", None),
        check_vma=False,
    )
```

time: 184 us -> 47.1 us (0.26)
  starting transfers between devices: 92.8 us -> 22.2 us
  waiting for transfers between devices: 33 us -> 0.01 us
  other arithmetic: 24.9 us -> 0 us
  blocking collectives: 26.1 us -> 9.85 us
  Pallas kernels: 0 us -> 14.8 us
  local copies, waits for them, and re-layouts: 5.16 us -> 0 us
    ppermute x16 -> x4, starting transfers between devices: 78.8 us -> 22.2 us  [the longest x1 11.9 us: shards(): east = lax.ppermute(to_west, 'space', [(b, a) for a, b in ring])]
    all_to_all x1 -> x0, waiting for transfers between devices: 24.1 us -> none  [shards(): lax.all_to_all(state, 'spec', split_axis=2, concat_axis=0, tiled=True)]
    mul x13 -> x0, other arithmetic: 21.1 us -> none  [the longest x8 18.5 us: update_once(): return (center - change) * sea]
    all_to_all x1, blocking collectives: 26.1 us -> 9.85 us  [shards(): pay = lax.all_to_all(pay, 'spec', split_axis=0, concat_axis=0, tiled=True)]
    pallas_call x0 -> x4, Pallas kernels: none -> 14.8 us  [the longest x1 6.91 us: inner(): pl.pallas_call(inner_kernel, in_specs=[WHOLE] * 4, out_specs=[WHOLE] * 6,...]
    all_to_all x1 -> x0, starting transfers between devices: 14 us -> none  [shards(): lax.all_to_all(state, 'spec', split_axis=2, concat_axis=0, tiled=True)]
    ppermute x16 -> x4, waiting for transfers between devices: 8.96 us -> 0.01 us  [the longest x1 0.01 us: shards(): west = lax.ppermute(to_east, 'space', ring)]
    slice x26 -> x0, local copies, waits for them, and re-layouts: 3.42 us -> none  [the longest x16 2.88 us: update_once(): after = jnp.roll(center, -1, axis=1)]
  transfers between devices with their start and end apart: 17 -> 4, of which waited for: 9 -> 0; matrix products, arithmetic and copies ran while one was open for 1% -> 0% of each run, Pallas kernels for 0% -> 15%
where the time goes in v1:
time: 47.1 us; the launch traced here: 46.9 us
  starting transfers between devices  22.2 us (47%)
  Pallas kernels  14.8 us (31%)
  blocking collectives  9.85 us (21%)
    ppermute x1, starting transfers between devices, shards(): east = lax.ppermute(to_west, 'space', [(b, a) for a, b in ring])  11.9 us
    all_to_all x1, blocking collectives, shards(): pay = lax.all_to_all(pay, 'spec', split_axis=0, concat_axis=0, tiled=True)  9.85 us
    pallas_call x1, Pallas kernels, inner(): pl.pallas_call(inner_kernel, in_specs=[WHOLE] * 4, out_specs=[WHOLE] * 6,...  6.91 us
    ppermute x1, starting transfers between devices, shards(): west = lax.ppermute(to_east, 'space', ring)  4.36 us
    pallas_call x1, Pallas kernels, strips(): pl.pallas_call(strips_kernel, in_specs=[WHOLE] * 13, out_specs=[WHOLE] *...  3.97 us
    ppermute x1, starting transfers between devices, shards(): lax.ppermute(far, 'spec', far_pairs + [(b, a) for a, b in far_pairs])  3.96 us
    pallas_call x1, Pallas kernels, pack(): pl.pallas_call(pack_kernel, in_specs=[SCALARS] + [in_hbm] * 5, out_specs=...  2.17 us
    ppermute x1, starting transfers between devices, shards(): lax.ppermute(near, 'spec', near_pairs + [(b, a) for a, b in near_pairs])  1.92 us
  transfers between devices with their start and end apart: 4, of which 0 were waited for; matrix products, arithmetic and copies ran while one was open for 0% of the time, Pallas kernels for 15%

profile of v1, /device:TPU:1, one launch (start us, length us, event | category | flops | bytes accessed | tf_op | source)
XLA Modules:
  0.0 46.9 jit_solution(10729455437603473228)
XLA Ops:
  0.0 2.2 %pack.1 = (f32[77,8,128]{2,1,0:T(8,128)S(1)}, f32[77,8,128]{2,1,0:T(8,128)S(1)}, f32[3,8,128]{2,1,0:T(8,128)S(1)}, f32[3,36,32,128]{3,2,1,0:T(8,128)S(1)}, f32[3...) custom-call(f32[3]{0:T(128)} %courant_ref.1, ...), custom_call_target="tpu_custom_call" | custom-call | tf_op jit(solution)/shard_map/pack/pallas_call | solution.py:86
  2.2 4.4 %collective-permute-start = (f32[77,8,128]{2,1,0:T(8,128)S(1)}, f32[77,8,128]{2,1,0:T(8,128)S(1)}, u32[]{:S(2)}, u32[]{:S(2)}) collective-permute-start(f32[77,8,128]{2,1,0:T(8,128)S(1)} %get-tuple-element.24), channel_id=1, source_target_pairs={{0,8},{8,16},{16,24},{24,32},{32,40},{40,48},{48,56},{56,64},{64,7... | collective-permute-start | bytes 946184 | tf_op jit(solution)/shard_map/ppermute | solution.py:386
  6.6 11.9 %collective-permute-start.1 = (f32[77,8,128]{2,1,0:T(8,128)S(1)}, f32[77,8,128]{2,1,0:T(8,128)S(1)}, u32[]{:S(2)}, u32[]{:S(2)}) collective-permute-start(f32[77,8,128]{2,1,0:T(8,128)S(1)} %get-tuple-element.25), channel_id=1, source_target_pairs={{8,0},{16,8},{24,16},{32,24},{40,32},{48,40},{56,48},{64,56},{72,6... | collective-permute-start | bytes 946184 | tf_op jit(solution)/shard_map/ppermute | solution.py:387
  18.5 6.9 %inner.1 = (f32[36,32,128]{2,1,0:T(8,128)S(1)}, f32[36,32,128]{2,1,0:T(8,128)S(1)}, f32[36,32,128]{2,1,0:T(8,128)S(1)}, f32[3,9,36,16,128]{4,3,2,1,0:T(8,128)S(1...) custom-call(f32[3,8,128]{2,1,0:T(8,128)S(1)} %get-tuple-element.23.speed_ref, ...), custom_call_target="tpu_custom_call" | custom-call | flops 40000000 | bytes 6000000 | tf_op jit(solution)/shard_map/inner/pallas_call | solution.py:193
  25.4 0.0 collective-permute-done.west_ref
  25.4 0.0 collective-permute-done.1.east_ref
  25.4 4.0 %strips.1 = (f32[36,32,128]{2,1,0:T(8,128)S(1)}, f32[36,32,128]{2,1,0:T(8,128)S(1)}, f32[36,32,128]{2,1,0:T(8,128)S(1)}, f32[3,9,36,16,128]{4,3,2,1,0:T(8,128)S(...) custom-call(f32[3,8,128]{2,1,0:T(8,128)S(1)} %get-tuple-element.23.s, ...), custom_call_target="tpu_custom_call", output_to_operand_aliasing={{0}: (7, {}), {1}: (8, {}), {2}: (9, {}), {3}: (10, {}), {4... | custom-call | tf_op jit(solution)/shard_map/strips/pallas_call | solution.py:291
  29.4 4.0 %collective-permute-start.2 = (f32[36,32,128]{2,1,0:T(8,128)S(1)}, f32[36,32,128]{2,1,0:T(8,128)S(1)}, u32[]{:S(2)}, u32[]{:S(2)}) collective-permute-start(f32[36,32,128]{2,1,0:T(8,128)S(1)} %get-tuple-element.37.far_ref), channel_id=1, source_target_pairs={{1,2},{3,4},{5,6},{2,1},{4,3},{6,5},{9,10},{11,12},{13,14},{10,9},... | collective-permute-start | bytes 1769480 | tf_op jit(solution)/shard_map/ppermute | solution.py:392
  33.4 1.9 %collective-permute-start.3 = (f32[36,32,128]{2,1,0:T(8,128)S(1)}, f32[36,32,128]{2,1,0:T(8,128)S(1)}, u32[]{:S(2)}, u32[]{:S(2)}) collective-permute-start(f32[36,32,128]{2,1,0:T(8,128)S(1)} %get-tuple-element.38.near_ref), channel_id=1, source_target_pairs={{0,1},{2,3},{4,5},{6,7},{1,0},{3,2},{5,4},{7,6},{8,9},{10,11},{12,... | collective-permute-start | bytes 1769480 | tf_op jit(solution)/shard_map/ppermute | solution.py:393
  35.3 9.8 %all_to_all.5.pay_ref = f32[8,40,128]{2,1,0:T(8,128)S(1)} all-to-all(f32[8,40,128]{2,1,0:T(8,128)S(1)} %get-tuple-element.40), channel_id=1, replica_groups=mesh['space'=64,'spec'=8] {'spec'}, dimensions={0} | all-to-all | bytes 327680 | tf_op jit(solution)/shard_map/all_to_all | solution.py:395
  45.2 0.0 collective-permute-done.2.far_in_ref
  45.2 0.0 collective-permute-done.3.near_in_ref
  45.2 1.7 %finish.1 = f32[3,36,32,128]{3,2,1,0:T(8,128)} custom-call(f32[36,32,128]{2,1,0:T(8,128)S(1)} %get-tuple-element.37.far_ref, f32[36,32,128]{2,1,0:T(8,128)S(1)} %get-tuple-element.38.near_ref, f32[36,32,128]{2,1,0:T(8,128)S(1)} %get-tuple-element.39.own_ref, f32[36,32,128]{2,1,0:T(8,128)S(1)} %collective-permute-done.2.far_in_ref, ...), custom_call_target="tpu_custom_call" | custom-call | tf_op jit(solution)/shard_map/finish/pallas_call | solution.py:366
Async XLA Ops:
  2.2 23.2 %collective-permute-start = (f32[77,8,128]{2,1,0:T(8,128)S(1)}, f32[77,8,128]{2,1,0:T(8,128)S(1)}, u32[]{:S(2)}, u32[]{:S(2)}) collective-permute-start(f32[77,8,128]{2,1,0:T(8,128)S(1)} %get-tuple-element.24), channel_id=1, source_target_pairs={{0,8},{8,16},{16,24},{24,32},{32,40},{40,48},{48,56},{56,64},{64,7... | collective-permute-start | bytes 946184 | tf_op jit(solution)/shard_map/ppermute | solution.py:386
  6.6 18.9 %collective-permute-start.1 = (f32[77,8,128]{2,1,0:T(8,128)S(1)}, f32[77,8,128]{2,1,0:T(8,128)S(1)}, u32[]{:S(2)}, u32[]{:S(2)}) collective-permute-start(f32[77,8,128]{2,1,0:T(8,128)S(1)} %get-tuple-element.25), channel_id=1, source_target_pairs={{8,0},{16,8},{24,16},{32,24},{40,32},{48,40},{56,48},{64,56},{72,6... | collective-permute-start | bytes 946184 | tf_op jit(solution)/shard_map/ppermute | solution.py:387
  29.4 15.7 %collective-permute-start.2 = (f32[36,32,128]{2,1,0:T(8,128)S(1)}, f32[36,32,128]{2,1,0:T(8,128)S(1)}, u32[]{:S(2)}, u32[]{:S(2)}) collective-permute-start(f32[36,32,128]{2,1,0:T(8,128)S(1)} %get-tuple-element.37.far_ref), channel_id=1, source_target_pairs={{1,2},{3,4},{5,6},{2,1},{4,3},{6,5},{9,10},{11,12},{13,14},{10,9},... | collective-permute-start | bytes 1769480 | tf_op jit(solution)/shard_map/ppermute | solution.py:392
  33.4 11.8 %collective-permute-start.3 = (f32[36,32,128]{2,1,0:T(8,128)S(1)}, f32[36,32,128]{2,1,0:T(8,128)S(1)}, u32[]{:S(2)}, u32[]{:S(2)}) collective-permute-start(f32[36,32,128]{2,1,0:T(8,128)S(1)} %get-tuple-element.38.near_ref), channel_id=1, source_target_pairs={{0,1},{2,3},{4,5},{6,7},{1,0},{3,2},{5,4},{7,6},{8,9},{10,11},{12,... | collective-permute-start | bytes 1769480 | tf_op jit(solution)/shard_map/ppermute | solution.py:393
